TPU v7x, 256 devices: a whole 4x4x8 slice. The times are simulated.
256 devices in a mesh: prow: 8 (over z), pcol: 32 (over x, y, core).
Axes of the slice: x: 4, y: 4, z: 8, core: 2. Of those that a mesh axis runs over, the one named last changes fastest.
Arguments:
- inverse_tiles: float32 [8192, 8192], P('pcol', 'prow'), may hold values from -6 to 6
- factor: float32 [2, 8192, 512], P(None, ('pcol', 'prow')), may hold values from -0.09375 to 0.09375
- link_factor: float32 [1, 512, 512], replicated, may hold values from -0.25 to 0.25
- diag_inverse: float32 [2, 512, 512], replicated, may hold values from -3 to 3
- ancestors: int32 [2, 8], replicated, may hold values from 0 to 15, as said below
Outputs:
- offdiag: float32 [2, 8192, 512], P(None, ('pcol', 'prow'))
- diag: float32 [2, 512, 512], P(None, 'pcol')
- link_blocks: float32 [1, 512, 512], P(None, 'pcol')
Inputs may be any that keep to these rules, and one draw needn't show every extreme that they name: `ancestors`: row k lists 8 distinct stored block rows; every row lists block 15, and row 0 lists block 0.
All inputs are finite; a program needn't handle non-finite values.
Results may differ from a plain program's by a relative error of at most 0.0001.
Values sent between devices are 32-bit elements; how exact they have to be, the bound alone decides.
A program may use at most 64 MiB of HBM per device.

v0:
```python
import jax
import jax.numpy as jnp
from jax import lax
from jax.sharding import PartitionSpec as P


def broadcast(value, axis, source):
    kept = jnp.where(lax.axis_index(axis) == source, value, 0).astype(value.dtype)
    return lax.psum(kept, axis)


def product(left_part, right_part):
    return jnp.dot(
        left_part, right_part, precision=lax.Precision.HIGHEST, preferred_element_type=jnp.float32
    )


def gather_columns(row_factor, ratio, prow_index, concat_dim):
    pieces = []
    for member in range(ratio):
        pieces.append(broadcast(row_factor, "pcol", prow_index * ratio + member))
    return jnp.concatenate(pieces, axis=concat_dim)


def body(inverse_tiles, factor, link_factor, diag_inverse, ancestors):
    row_count, col_count = inverse_tiles.shape
    nsuper, unit_rows, columns = factor.shape
    prow_count = lax.axis_size("prow")
    pcol_count = lax.axis_size("pcol")
    ratio = col_count // row_count
    prow_index = lax.axis_index("prow")
    pcol_index = lax.axis_index("pcol")
    first_row = (pcol_index * prow_count + prow_index) * unit_rows
    block_ids = (first_row + lax.iota(jnp.int32, unit_rows)) // columns
    selected = jnp.any(block_ids[None, :, None] == ancestors[:, None, :], axis=2).astype(
        jnp.float32
    )
    unit_factor = factor * selected[:, :, None]
    slice_rows = columns // pcol_count
    slice_start = pcol_index * slice_rows
    offdiag_list = []
    diag_list = []
    link_list = []
    prior_offdiag = None
    prior_diag = None
    for number in range(nsuper):
        row_factor = lax.all_gather(unit_factor[number], "prow", axis=0, tiled=True)
        col_factor = gather_columns(row_factor, ratio, prow_index, 0)

        def partial_term(begin_row, row_total, col_factor=col_factor):
            return product(inverse_tiles, col_factor)

        summed = lax.psum_scatter(
            partial_term(jnp.int32(0), lax.axis_size("prow") * unit_rows),
            "prow",
            scatter_dimension=0,
            tiled=True,
        )
        local_factor = unit_factor[number]
        gram_part = product(local_factor.T, summed)
        keep_rows = selected[number][:, None]
        if number == 0:
            gram_sum = lax.psum(gram_part, ("prow", "pcol"))
            result = -(keep_rows * summed)
            diag_block = diag_inverse[0] + gram_sum
        else:
            link_block = link_factor[number - 1]
            cross_part = product(prior_offdiag.T, local_factor)
            gram_sum, cross_sum = lax.psum((gram_part, cross_part), ("prow", "pcol"))
            result = -(keep_rows * (summed + product(prior_offdiag, link_block)))
            link_out = -(cross_sum + product(prior_diag, link_block))
            diag_block = (
                diag_inverse[number]
                + gram_sum
                + product(cross_sum.T, link_block)
                - product(link_block.T, link_out)
            )
            link_list.append(lax.dynamic_slice_in_dim(link_out, slice_start, slice_rows, 0))
        offdiag_list.append(result)
        diag_list.append(lax.dynamic_slice_in_dim(diag_block, slice_start, slice_rows, 0))
        prior_offdiag = result
        prior_diag = diag_block
    return (jnp.stack(offdiag_list), jnp.stack(diag_list), jnp.stack(link_list))


def solution(mesh):
    in_specs = (P("pcol", "prow"), P(None, ("pcol", "prow"), None), P(), P(), P())
    out_specs = (P(None, ("pcol", "prow"), None), P(None, "pcol", None), P(None, "pcol", None))
    return jax.shard_map(body, mesh=mesh, in_specs=in_specs, out_specs=out_specs, check_vma=False)
```

profile of v0, /device:TPU:2, one launch (start us, length us, event | category | flops | bytes accessed | tf_op | source)
XLA Modules:
  0.0 558.0 jit_solution(3136330771844192)
XLA Ops:
  8.1 1.0 broadcast_multiply_fusion
  9.1 29.1 %all-gather = f32[1,256,512]{2,1,0:T(8,128)S(1)} all-gather(f32[1,32,512]{2,1,0:T(8,128)S(1)} %get-tuple-element.25), channel_id=2, replica_groups=mesh['prow'=8,'pcol'=32] {'prow'}, dimensions={1}, use_global_device_ids=true | all-gather | bytes 589824 | tf_op jit(solution)/shard_map/all_gather | solution.py:47
  38.2 25.6 %all-gather.1 = f32[1,256,512]{2,1,0:T(8,128)S(1)} all-gather(f32[1,32,512]{2,1,0:T(8,128)S(1)} %get-tuple-element.26), channel_id=3, replica_groups=mesh['prow'=8,'pcol'=32] {'prow'}, dimensions={1}, use_global_device_ids=true | all-gather | bytes 589824 | tf_op jit(solution)/shard_map/all_gather | solution.py:47
  63.8 1.4 select_bitcast_fusion.7
  65.3 1.4 select_bitcast_fusion.3
  66.8 121.3 %all-reduce.7.cloned.1.call-done = (f32[256,512]{1,0:T(8,128)}, f32[256,512]{1,0:T(8,128)}, f32[256,512]{1,0:T(8,128)}, f32[256,512]{1,0:T(8,128)}, f32[256,512]...) async-done(((f32[256,512]{1,0:T(8,128)}, f32[256,512]{1,0:T(8,128)}, f32[256,512]{1,0:T(8,128)}, f32[256,512]{1,0:T(8,128)}, ...) | async-done | bytes 4194320 | tf_op jit(solution)/shard_map/psum | solution.py:9
  188.1 5.0 fusion.20
  193.1 1.0 copy.14
  194.2 4.8 fusion.17
  199.0 1.0 copy.16
  200.3 31.7 %reduce-scatter.7.cloned.1.call-done = f32[32,512]{1,0:T(8,128)} async-done(((f32[256,512]{1,0:T(8,128)}), f32[32,512]{1,0:T(8,128)}) %reduce-scatter.7.cloned.1.call-update) | async-done | bytes 65552
  231.9 1.0 copy.15
  232.9 2.8 fusion.38
  235.7 2.0 fusion.31
  237.7 33.2 %reduce-scatter.9.cloned.1.call-done = f32[32,512]{1,0:T(8,128)} async-done(((f32[256,512]{1,0:T(8,128)}), f32[32,512]{1,0:T(8,128)}) %reduce-scatter.9.cloned.1.call-update) | async-done | bytes 65552
  270.9 2.9 fusion.35
  273.8 1.1 slice_bitcast_fusion
  275.6 1.0 copy.13
  278.0 264.3 %all-reduce.5.cloned.1.call-done = (f32[512,512]{1,0:T(8,128)}, f32[512,512]{1,0:T(8,128)}, f32[512,512]{1,0:T(8,128)}) async-done(((f32[512,512]{1,0:T(8,128)}, f32[512,512]{1,0:T(8,128)}, f32[512,512]{1,0:T(8,128)}), (f32[512,512]{1,0:T(8,128)}, f32[512,512]{1,0:T(8,128)}, f32[512,512]{1,0:T(8,128)})) %all-reduce.5.cloned.1.call-update) | async-done | bytes 3145744 | tf_op jit(solution)/shard_map/psum | solution.py:69
  542.3 1.5 bitcast_add_fusion
  543.8 1.9 fusion.28
  545.7 1.9 fusion.16
  547.5 1.9 convolution_bitcast_fusion
  549.5 1.4 fusion.40
  (30 shorter events, 4.0 us)
Async XLA Ops:
  7.2 269.5 %copy-start = (f32[1,512,512]{2,1,0:T(8,128)S(1)}, f32[1,512,512]{2,1,0:T(8,128)}, u32[]{:S(2)}) copy-start(f32[1,512,512]{2,1,0:T(8,128)} %param.7) | copy-start | bytes 3145732
  7.2 180.9 %all-reduce.7.cloned.1.call-start = ((), (), s32[]{:S(2)}) async-start(), calls=%async_computation.5 | async-start | bytes 8388608 | tf_op jit(solution)/shard_map/psum | solution.py:9
  66.7 121.4 %copy-start.4 = (f32[256,1024]{1,0:T(8,128)S(1)}, f32[256,1024]{1,0:T(8,128)}, u32[]{:S(2)}) copy-start(f32[256,1024]{1,0:T(8,128)} %param.5) | copy-start | bytes 3145732
  66.7 165.2 %reduce-scatter.7.cloned.1.call-start = ((), (), s32[]{:S(2)}) async-start(), calls=%async_computation.2 | async-start | bytes 589824
  188.1 6.1 %copy-start.5 = (f32[256,512]{1,0:T(8,128)S(1)}, f32[256,512]{1,0:T(8,128)}, u32[]{:S(2)}) copy-start(f32[256,512]{1,0:T(8,128)} %get-tuple-element.9) | copy-start | bytes 1572868
  194.1 76.8 %reduce-scatter.9.cloned.1.call-start = ((), (), s32[]{:S(2)}) async-start(), calls=%async_computation.3 | async-start | bytes 589824
  200.0 342.3 %all-reduce.5.cloned.1.call-start = ((), (), s32[]{:S(2)}) async-start(), calls=%async_computation.4 | async-start | bytes 6291456 | tf_op jit(solution)/shard_map/psum | solution.py:69
  237.7 36.1 %copy-start.2 = (f32[2,512,512]{2,1,0:T(8,128)S(1)}, f32[2,512,512]{2,1,0:T(8,128)}, u32[]{:S(2)}) copy-start(f32[2,512,512]{2,1,0:T(8,128)} %param.8) | copy-start | bytes 6291460
  273.8 2.8 copy-start.3
  542.3 1.5 copy-start.1
Sparse Core Ops, SparseCore 0:
  66.8 121.1 all-reduce.6
  194.2 37.6 reduce-scatter.6
  234.5 36.4 reduce-scatter.8
  276.5 265.7 all-reduce.4
where the time goes:
time: 558 us
  waiting for transfers between devices  450 us (81%)
  blocking collectives  54.7 us (10%)
  matrix products  23.8 us (4%)
  between operations  13.9 us (2%)
  other arithmetic  9.63 us (2%)
    psum x1, waiting for transfers between devices, body(): gram_sum, cross_sum = lax.psum((gram_part, cross_part), ('prow', 'pcol'))  264 us
    psum x1, waiting for transfers between devices, broadcast(): return lax.psum(kept, axis)  121 us
    unnamed x6, waiting for transfers between devices  64.9 us
    all_gather x2, blocking collectives, body(): row_factor = lax.all_gather(unit_factor[number], 'prow', axis=0, tiled=True)  54.7 us
    dot_general x9, matrix products, product(): jnp.dot(left_part, right_part, precision=lax.Precision.HIGHEST, preferred...  23.8 us
  transfers between devices with their start and end apart: 4, of which 4 were waited for; matrix products, arithmetic and copies ran while one was open for 3% of the time, Pallas kernels for 0%

commit v1 on v0

--- a/solution.py
+++ b/solution.py
@@ -2,6 +2,7 @@
 import jax.numpy as jnp
 from jax import lax
 from jax.sharding import PartitionSpec as P
+from jax.lax import psum
 
 
 def broadcast(value, axis, source):
@@ -66,7 +67,7 @@
         else:
             link_block = link_factor[number - 1]
             cross_part = product(prior_offdiag.T, local_factor)
-            gram_sum, cross_sum = lax.psum((gram_part, cross_part), ("prow", "pcol"))
+            gram_sum, cross_sum = psum(psum((gram_part, cross_part), "pcol"), "prow")
             result = -(keep_rows * (summed + product(prior_offdiag, link_block)))
             link_out = -(cross_sum + product(prior_diag, link_block))
             diag_block = (

time: 558 us -> 754 us (1.35)
  waiting for transfers between devices: 450 us -> 645 us
    psum x1 -> x3, waiting for transfers between devices: 264 us -> 456 us  [the longest x1 262 us: body(): gram_sum = lax.psum(gram_part, ('prow', 'pcol'))]
    unnamed x6 -> x8, waiting for transfers between devices: 64.9 us -> 68 us
  transfers between devices with their start and end apart: 4 -> 6, of which waited for: 4 -> 6; matrix products, arithmetic and copies ran while one was open for 3% -> 2% of each run, Pallas kernels for 0% -> 0%
where the time goes in v1:
time: 754 us
  waiting for transfers between devices  645 us (86%)
  blocking collectives  54.7 us (7%)
  matrix products  25.2 us (3%)
  between operations  14.3 us (2%)
  other arithmetic  9.2 us (1%)
    psum x1, waiting for transfers between devices, body(): gram_sum = lax.psum(gram_part, ('prow', 'pcol'))  262 us
    psum x2, waiting for transfers between devices, body(): gram_sum, cross_sum = psum(psum((gram_part, cross_part), 'pcol'), 'prow')  194 us
    psum x1, waiting for transfers between devices, broadcast(): return lax.psum(kept, axis)  121 us
    unnamed x8, waiting for transfers between devices  68 us
    all_gather x2, blocking collectives, body(): row_factor = lax.all_gather(unit_factor[number], 'prow', axis=0, tiled=True)  54.7 us
    dot_general x9, matrix products, product(): jnp.dot(left_part, right_part, precision=lax.Precision.HIGHEST, preferred...  25.2 us
  transfers between devices with their start and end apart: 6, of which 6 were waited for; matrix products, arithmetic and copies ran while one was open for 2% of the time, Pallas kernels for 0%

profile of v1, /device:TPU:2, one launch (start us, length us, event | category | flops | bytes accessed | tf_op | source)
XLA Modules:
  0.0 753.5 jit_solution(9574245205419443425)
XLA Ops:
  8.1 1.0 broadcast_multiply_fusion
  9.1 29.1 %all-gather = f32[1,256,512]{2,1,0:T(8,128)S(1)} all-gather(f32[1,32,512]{2,1,0:T(8,128)S(1)} %get-tuple-element.26), channel_id=2, replica_groups=mesh['prow'=8,'pcol'=32] {'prow'}, dimensions={1}, use_global_device_ids=true | all-gather | bytes 589824 | tf_op jit(solution)/shard_map/all_gather | solution.py:48
  38.2 25.6 %all-gather.1 = f32[1,256,512]{2,1,0:T(8,128)S(1)} all-gather(f32[1,32,512]{2,1,0:T(8,128)S(1)} %get-tuple-element.27), channel_id=3, replica_groups=mesh['prow'=8,'pcol'=32] {'prow'}, dimensions={1}, use_global_device_ids=true | all-gather | bytes 589824 | tf_op jit(solution)/shard_map/all_gather | solution.py:48
  63.8 1.4 select_bitcast_fusion.7
  65.3 1.4 select_bitcast_fusion.3
  66.8 121.3 %all-reduce.12.cloned.1.call-done = (f32[256,512]{1,0:T(8,128)}, f32[256,512]{1,0:T(8,128)}, f32[256,512]{1,0:T(8,128)}, f32[256,512]{1,0:T(8,128)}, f32[256,512...) async-done(((f32[256,512]{1,0:T(8,128)}, f32[256,512]{1,0:T(8,128)}, f32[256,512]{1,0:T(8,128)}, f32[256,512]{1,0:T(8,128)}, ...) | async-done | bytes 4194320 | tf_op jit(solution)/shard_map/psum | solution.py:10
  188.1 5.0 fusion.20
  193.1 1.0 copy.14
  194.2 4.8 fusion.17
  199.0 1.0 copy.16
  200.1 31.8 %reduce-scatter.7.cloned.1.call-done = f32[32,512]{1,0:T(8,128)} async-done(((f32[256,512]{1,0:T(8,128)}), f32[32,512]{1,0:T(8,128)}) %reduce-scatter.7.cloned.1.call-update) | async-done | bytes 65552
  232.9 1.9 fusion.31
  234.8 36.1 %reduce-scatter.9.cloned.1.call-done = f32[32,512]{1,0:T(8,128)} async-done(((f32[256,512]{1,0:T(8,128)}), f32[32,512]{1,0:T(8,128)}) %reduce-scatter.9.cloned.1.call-update) | async-done | bytes 65552
  270.9 2.9 fusion.35
  273.9 3.0 fusion.38
  277.1 112.6 %all-reduce.10.cloned.1.call-done = (f32[512,512]{1,0:T(8,128)}, f32[512,512]{1,0:T(8,128)}) async-done(((f32[512,512]{1,0:T(8,128)}, f32[512,512]{1,0:T(8,128)}), (f32[512,512]{1,0:T(8,128)}, f32[512,512]{1,0:T(8,128)})) %all-reduce.10.cloned.1.call-update) | async-done | bytes 2097168 | tf_op jit(solution)/shard_map/psum | solution.py:70
  389.7 1.1 slice_bitcast_fusion
  392.3 262.0 %all-reduce.8.cloned.1.call-done = f32[512,512]{1,0:T(8,128)} async-done(((f32[512,512]{1,0:T(8,128)}), f32[512,512]{1,0:T(8,128)}) %all-reduce.8.cloned.1.call-update) | async-done | bytes 1048592 | tf_op jit(solution)/shard_map/psum | solution.py:64
  654.3 1.7 bitcast_add_fusion
  656.1 81.6 %all-reduce.14.cloned.1.call-done = (f32[512,512]{1,0:T(8,128)}, f32[512,512]{1,0:T(8,128)}) async-done(((f32[512,512]{1,0:T(8,128)}, f32[512,512]{1,0:T(8,128)}), (f32[512,512]{1,0:T(8,128)}, f32[512,512]{1,0:T(8,128)})) %all-reduce.14.cloned.1.call-update) | async-done | bytes 2097168 | tf_op jit(solution)/shard_map/psum | solution.py:70
  737.7 3.2 fusion.16
  740.9 1.8 fusion.28
  742.8 1.9 convolution_bitcast_fusion
  744.6 1.4 fusion.40
  (36 shorter events, 4.5 us)
Async XLA Ops:
  7.2 383.8 %copy-start = (f32[1,512,512]{2,1,0:T(8,128)S(1)}, f32[1,512,512]{2,1,0:T(8,128)}, u32[]{:S(2)}) copy-start(f32[1,512,512]{2,1,0:T(8,128)} %param.7) | copy-start | bytes 3145732
  7.2 180.9 %all-reduce.12.cloned.1.call-start = ((), (), s32[]{:S(2)}) async-start(), calls=%async_computation.6 | async-start | bytes 8388608 | tf_op jit(solution)/shard_map/psum | solution.py:10
  66.7 121.4 %copy-start.4 = (f32[256,1024]{1,0:T(8,128)S(1)}, f32[256,1024]{1,0:T(8,128)}, u32[]{:S(2)}) copy-start(f32[256,1024]{1,0:T(8,128)} %param.5) | copy-start | bytes 3145732
  66.7 165.2 %reduce-scatter.7.cloned.1.call-start = ((), (), s32[]{:S(2)}) async-start(), calls=%async_computation.3 | async-start | bytes 589824
  188.1 6.1 copy-start.5
  194.1 76.8 %reduce-scatter.9.cloned.1.call-start = ((), (), s32[]{:S(2)}) async-start(), calls=%async_computation.4 | async-start | bytes 589824
  200.0 189.7 %all-reduce.10.cloned.1.call-start = ((), (), s32[]{:S(2)}) async-start(), calls=%async_computation.5 | async-start | bytes 4194304 | tf_op jit(solution)/shard_map/psum | solution.py:70
  273.8 115.9 %copy-start.2 = (f32[2,512,512]{2,1,0:T(8,128)S(1)}, f32[2,512,512]{2,1,0:T(8,128)}, u32[]{:S(2)}) copy-start(f32[2,512,512]{2,1,0:T(8,128)} %param.8) | copy-start | bytes 6291460
  273.8 380.5 %all-reduce.8.cloned.1.call-start = ((), (), s32[]{:S(2)}) async-start(), calls=%async_computation.2 | async-start | bytes 2097152 | tf_op jit(solution)/shard_map/psum | solution.py:64
  276.9 460.8 %all-reduce.14.cloned.1.call-start = ((), (), s32[]{:S(2)}) async-start(), calls=%async_computation.7 | async-start | bytes 4194304 | tf_op jit(solution)/shard_map/psum | solution.py:70
  389.7 1.2 copy-start.3
  737.7 3.2 copy-start.1
Sparse Core Ops, SparseCore 0:
  66.9 121.1 all-reduce.11
  194.3 37.6 reduce-scatter.6
  234.4 36.4 reduce-scatter.8
  274.1 115.5 all-reduce.9
  395.0 259.2 all-reduce.7
  656.6 81.1 all-reduce.13
